TPU v7x, 32 devices: a whole 2x2x4 slice. The times are simulated.
32 devices in a mesh: dp: 8 (over z, y), mp: 4 (over x, core).
Axes of the slice: x: 2, y: 2, z: 4, core: 2. Of those that a mesh axis runs over, the one named last changes fastest.
Arguments:
- tokens: bfloat16 [16384, 768], P(('dp', 'mp')), may hold values from -6 to 6
- doc_lengths: int32 [8, 4], P('dp'), may hold values from 1 to 1024, 1792 in all within a row
- attn_gain: float32 [768], replicated, may hold values from 0.5 to 1.5
- attn_shift: float32 [768], replicated, may hold values from -1.75 to 1.75
- query_weight: bfloat16 [768, 768], P(None, 'mp'), may hold values from -0.21875 to 0.21875
- query_bias: float32 [768], P('mp'), may hold values from -1.75 to 1.75
- key_weight: bfloat16 [768, 64], replicated, may hold values from -0.21875 to 0.21875
- key_bias: float32 [64], replicated, may hold values from -3 to 3
- value_weight: bfloat16 [768, 64], replicated, may hold values from -0.21875 to 0.21875
- value_bias: float32 [64], replicated, may hold values from -1.75 to 1.75
- out_weight: bfloat16 [768, 768], P('mp'), may hold values from -0.875 to 0.875
- out_bias: float32 [768], replicated, may hold values from -1.75 to 1.75
- mlp_gain: float32 [768], replicated, may hold values from 0.5 to 1.5
- mlp_shift: float32 [768], replicated, may hold values from -1.75 to 1.75
- up_weight: bfloat16 [768, 3072], P(None, 'mp'), may hold values from -0.21875 to 0.21875
- up_bias: float32 [3072], P('mp'), may hold values from -1.75 to 1.75
- down_weight: bfloat16 [3072, 768], P('mp'), may hold values from -0.21875 to 0.21875
- down_bias: float32 [768], replicated, may hold values from -1.75 to 1.75
- out_grad: bfloat16 [16384, 768], P(('dp', 'mp')), may hold values from -6 to 6
Outputs:
- block_out: bfloat16 [16384, 768], P(('dp', 'mp'))
- input_grad: bfloat16 [16384, 768], P(('dp', 'mp'))
- attn_gain_grad: float32 [768], replicated
- attn_shift_grad: float32 [768], replicated
- query_weight_grad: float32 [768, 768], P(None, 'mp')
- query_bias_grad: float32 [768], P('mp')
- key_weight_grad: float32 [768, 64], replicated
- key_bias_grad: float32 [64], replicated
- value_weight_grad: float32 [768, 64], replicated
- value_bias_grad: float32 [64], replicated
- out_weight_grad: float32 [768, 768], P('mp')
- out_bias_grad: float32 [768], replicated
- mlp_gain_grad: float32 [768], replicated
- mlp_shift_grad: float32 [768], replicated
- up_weight_grad: float32 [768, 3072], P(None, 'mp')
- up_bias_grad: float32 [3072], P('mp')
- down_weight_grad: float32 [3072, 768], P('mp')
- down_bias_grad: float32 [768], replicated
All inputs are finite; a program needn't handle non-finite values.
Results may differ from a plain program's by a relative error of at most 0.02.
Values may be sent and summed in bfloat16 or wider, within the bound.
A program may use at most 128 MiB of HBM per device.

v0:
```python
from functools import partial
import jax
import jax.numpy as jnp
from jax import lax
from jax.sharding import PartitionSpec as P

HD = 64
ROT = 16
SLOT = 2048
DOCS = 4
epsilon = 1e-05


def normalize(values):
    average = jnp.mean(values, axis=-1, keepdims=True)
    centered = values - average
    inv_std = lax.rsqrt(jnp.mean(centered * centered, axis=-1, keepdims=True) + epsilon)
    return (centered * inv_std, inv_std)


def rotate(values, cos_table, sine_table):
    half_rot = ROT // 2
    lower_part = values[..., :half_rot]
    upper_part = values[..., half_rot:ROT]
    return jnp.concatenate(
        [
            lower_part * cos_table - upper_part * sine_table,
            upper_part * cos_table + lower_part * sine_table,
            values[..., ROT:],
        ],
        axis=-1,
    )


def row_layout(lengths):
    slot_index = jnp.arange(SLOT, dtype=jnp.int32)
    doc_ends = jnp.cumsum(lengths, axis=-1)
    doc_starts = doc_ends - lengths
    segment = jnp.sum((slot_index[:, None] >= doc_ends[..., None, :]).astype(jnp.int32), axis=-1)
    doc_begins = jnp.concatenate([doc_starts, doc_ends[..., -1:]], axis=-1)
    labels = jnp.arange(DOCS + 1, dtype=jnp.int32)
    picked = jnp.sum(jnp.where(segment[..., None] == labels, doc_begins[..., None, :], 0), axis=-1)
    return (segment, slot_index - picked)


def angles(position):
    half_rot = ROT // 2
    frequency = 10000.0 ** (-(2.0 * jnp.arange(half_rot, dtype=jnp.float32)) / ROT)
    angle_grid = position.astype(jnp.float32)[..., None] * frequency
    return (jnp.cos(angle_grid), jnp.sin(angle_grid))


def inner_rows(left, right):
    return lax.dot_general(
        left, right, (((0,), (0,)), ((), ())), preferred_element_type=jnp.float32
    )


def times_transposed(left, right):
    return lax.dot_general(
        left, right, (((1,), (1,)), ((), ())), preferred_element_type=jnp.float32
    )


def block_scores(query_block, key_row, seg_row, first_row):
    block_rows = query_block.shape[0]
    scores = jnp.einsum(
        "bhe,ke->hbk", query_block, key_row, preferred_element_type=jnp.float32
    ) * HD ** (-0.5)
    query_index = first_row + jnp.arange(block_rows, dtype=jnp.int32)
    key_index = jnp.arange(SLOT, dtype=jnp.int32)
    seg_rows = lax.dynamic_slice_in_dim(seg_row, first_row, block_rows)
    allowed = (seg_rows[:, None] == seg_row[None, :]) & (key_index[None, :] <= query_index[:, None])
    return (scores, allowed)


def attend_forward(queries, key_rows, value_rows, segment):
    total_rows, heads = (queries.shape[0], queries.shape[1])
    groups = total_rows // SLOT
    block_rows = min(512, SLOT)
    block_count = SLOT // block_rows
    key_groups = key_rows.reshape(groups, SLOT, HD)
    value_groups = value_rows.reshape(groups, SLOT, HD)

    def one_block(block_item):
        query_block, item_index = block_item
        row_index = item_index // block_count
        first_row = item_index % block_count * block_rows
        key_row = lax.dynamic_index_in_dim(key_groups, row_index, 0, keepdims=False)
        value_row = lax.dynamic_index_in_dim(value_groups, row_index, 0, keepdims=False)
        seg_row = lax.dynamic_index_in_dim(segment, row_index, 0, keepdims=False)
        scores, allowed = block_scores(query_block, key_row, seg_row, first_row)
        scores = jnp.where(allowed[None], scores, -1e30)
        peak = jnp.max(scores, axis=-1, keepdims=True)
        expo = jnp.exp(scores - peak)
        totals = jnp.sum(expo, axis=-1, keepdims=True)
        probs_low = (expo / totals).astype(jnp.bfloat16)
        context = jnp.einsum(
            "hbk,ke->bhe", probs_low, value_row, preferred_element_type=jnp.float32
        )
        return (context, (peak + jnp.log(totals))[..., 0])

    item_list = jnp.arange(groups * block_count, dtype=jnp.int32)
    context, summary = lax.map(
        one_block, (queries.reshape(groups * block_count, block_rows, heads, HD), item_list)
    )
    return (context.reshape(total_rows, heads * HD), summary)


def attend_backward(queries, key_rows, value_rows, segment, summary, context_grad):
    total_rows, heads = (queries.shape[0], queries.shape[1])
    groups = total_rows // SLOT
    block_rows = min(512, SLOT)
    block_count = SLOT // block_rows
    key_groups = key_rows.reshape(groups, SLOT, HD)
    value_groups = value_rows.reshape(groups, SLOT, HD)

    def one_block(block_item):
        query_block, grad_block, summary_block, item_index = block_item
        row_index = item_index // block_count
        first_row = item_index % block_count * block_rows
        key_row = lax.dynamic_index_in_dim(key_groups, row_index, 0, keepdims=False)
        value_row = lax.dynamic_index_in_dim(value_groups, row_index, 0, keepdims=False)
        seg_row = lax.dynamic_index_in_dim(segment, row_index, 0, keepdims=False)
        scores, allowed = block_scores(query_block, key_row, seg_row, first_row)
        probs = jnp.where(allowed[None], jnp.exp(scores - summary_block[..., None]), 0.0)
        probs_low = probs.astype(jnp.bfloat16)
        prob_grad = jnp.einsum(
            "bhe,ke->hbk", grad_block, value_row, preferred_element_type=jnp.float32
        )
        delta = jnp.sum(probs * prob_grad, axis=-1, keepdims=True)
        score_grad = (probs * (prob_grad - delta)).astype(jnp.bfloat16)
        query_part = jnp.einsum(
            "hbk,ke->bhe", score_grad, key_row, preferred_element_type=jnp.float32
        ) * HD ** (-0.5)
        key_part = jnp.einsum(
            "hbk,bhe->ke", score_grad, query_block, preferred_element_type=jnp.float32
        ) * HD ** (-0.5)
        value_part = jnp.einsum(
            "hbk,bhe->ke", probs_low, grad_block, preferred_element_type=jnp.float32
        )
        return (query_part, key_part, value_part)

    item_list = jnp.arange(groups * block_count, dtype=jnp.int32)
    query_part, key_part, value_part = lax.map(
        one_block,
        (
            queries.reshape(groups * block_count, block_rows, heads, HD),
            context_grad.reshape(groups * block_count, block_rows, heads, HD),
            summary,
            item_list,
        ),
    )
    key_grad = jnp.sum(key_part.reshape(groups, block_count, SLOT, HD), axis=1).reshape(
        total_rows, HD
    )
    value_grad = jnp.sum(value_part.reshape(groups, block_count, SLOT, HD), axis=1).reshape(
        total_rows, HD
    )
    return (query_part.reshape(total_rows, heads, HD), key_grad, value_grad)


def forward_local(gathered, segment, cos_table, sine_table, local_weights):
    (
        attn_gain,
        attn_shift,
        query_weight,
        query_bias,
        key_weight,
        key_bias,
        value_weight,
        value_bias,
        mlp_gain,
        mlp_shift,
        up_weight,
        up_bias,
    ) = local_weights
    total_rows = gathered.shape[0]
    heads = query_weight.shape[1] // HD
    normed, unused_std = normalize(gathered.astype(jnp.float32))
    attn_in = (normed * attn_gain + attn_shift).astype(jnp.bfloat16)
    mlp_in = (normed * mlp_gain + mlp_shift).astype(jnp.bfloat16)
    queries = jnp.dot(attn_in, query_weight, preferred_element_type=jnp.float32) + query_bias
    queries = rotate(
        queries.reshape(total_rows, heads, HD), cos_table[:, None, :], sine_table[:, None, :]
    ).astype(jnp.bfloat16)
    key_value = jnp.dot(
        attn_in,
        jnp.concatenate([key_weight, value_weight], axis=1),
        preferred_element_type=jnp.float32,
    )
    key_value = key_value + jnp.concatenate([key_bias, value_bias])
    key_rows = rotate(key_value[:, :HD], cos_table, sine_table).astype(jnp.bfloat16)
    value_rows = key_value[:, HD:].astype(jnp.bfloat16)
    context, summary = attend_forward(queries, key_rows, value_rows, segment)
    context = context.astype(jnp.bfloat16)
    hidden_pre = jnp.dot(mlp_in, up_weight, preferred_element_type=jnp.float32) + up_bias
    hidden = jax.nn.gelu(hidden_pre, approximate=False).astype(jnp.bfloat16)
    return (
        attn_in,
        mlp_in,
        queries,
        key_rows,
        value_rows,
        context,
        summary,
        hidden_pre,
        hidden,
        normed,
    )


def per_device(
    tokens,
    doc_lengths,
    attn_gain,
    attn_shift,
    query_weight,
    query_bias,
    key_weight,
    key_bias,
    value_weight,
    value_bias,
    out_weight,
    out_bias,
    mlp_gain,
    mlp_shift,
    up_weight,
    up_bias,
    down_weight,
    down_bias,
    out_grad,
):
    shard_rows = tokens.shape[0]
    my_first = lax.axis_index("mp") * shard_rows
    segment, position = row_layout(doc_lengths)
    cos_table, sine_table = angles(position.reshape(-1))
    shard_valid = lax.dynamic_slice_in_dim(segment.reshape(-1), my_first, shard_rows) < DOCS
    local_weights = (
        attn_gain,
        attn_shift,
        query_weight,
        query_bias,
        key_weight,
        key_bias,
        value_weight,
        value_bias,
        mlp_gain,
        mlp_shift,
        up_weight,
        up_bias,
    )
    gathered = lax.all_gather(tokens, "mp", axis=0, tiled=True)
    kept = forward_local(gathered, segment, cos_table, sine_table, local_weights)
    context_fwd, hidden_fwd = (kept[5], kept[8])
    branch_sum = lax.psum_scatter(
        jnp.dot(context_fwd, out_weight, preferred_element_type=jnp.float32)
        + jnp.dot(hidden_fwd, down_weight, preferred_element_type=jnp.float32),
        "mp",
        scatter_dimension=0,
        tiled=True,
    )
    token_values = tokens.astype(jnp.float32)
    block_out = (token_values + branch_sum + out_bias + down_bias).astype(jnp.bfloat16)
    grad_shard = out_grad * shard_valid[:, None].astype(jnp.bfloat16)
    regathered = lax.all_gather(tokens, "mp", axis=0, tiled=True)
    kept = forward_local(regathered, segment, cos_table, sine_table, local_weights)
    (
        attn_in,
        mlp_in,
        queries,
        key_rows,
        value_rows,
        context,
        summary,
        hidden_pre,
        hidden,
        normed_all,
    ) = kept
    grad_rows = lax.all_gather(grad_shard, "mp", axis=0, tiled=True)
    out_weight_grad = inner_rows(context, grad_rows)
    down_weight_grad = inner_rows(hidden, grad_rows)
    bias_grad = jnp.sum(grad_shard, axis=0, dtype=jnp.float32)
    context_grad = times_transposed(grad_rows, out_weight).astype(jnp.bfloat16)
    hidden_grad = times_transposed(grad_rows, down_weight)
    unused_out, gelu_pull = jax.vjp(partial(jax.nn.gelu, approximate=False), hidden_pre)
    pre_grad = gelu_pull(hidden_grad)[0].astype(jnp.bfloat16)
    up_weight_grad = inner_rows(mlp_in, pre_grad)
    up_bias_grad = jnp.sum(pre_grad, axis=0, dtype=jnp.float32)
    mlp_part = times_transposed(pre_grad, up_weight)
    query_grad, key_part, value_part = attend_backward(
        queries, key_rows, value_rows, segment, summary, context_grad
    )
    total_rows = query_grad.shape[0]
    query_grad = (
        rotate(query_grad, cos_table[:, None, :], -sine_table[:, None, :])
        .reshape(total_rows, -1)
        .astype(jnp.bfloat16)
    )
    key_part = rotate(key_part, cos_table, -sine_table)
    query_weight_grad = inner_rows(attn_in, query_grad)
    query_bias_grad = jnp.sum(query_grad, axis=0, dtype=jnp.float32)
    attn_part = times_transposed(query_grad, query_weight)
    normed, inv_std = normalize(token_values)
    attn_rows = lax.dynamic_slice_in_dim(attn_in, my_first, shard_rows)
    attn_grad, mlp_grad, key_grad, value_grad = (
        lax.psum_scatter(attn_part, "mp", scatter_dimension=0, tiled=True),
        lax.psum_scatter(mlp_part, "mp", scatter_dimension=0, tiled=True),
        lax.psum_scatter(key_part, "mp", scatter_dimension=0, tiled=True),
        lax.psum_scatter(value_part, "mp", scatter_dimension=0, tiled=True),
    )
    key_low = key_grad.astype(jnp.bfloat16)
    value_low = value_grad.astype(jnp.bfloat16)
    attn_grad = (
        attn_grad
        + times_transposed(key_low, key_weight)
        + times_transposed(value_low, value_weight)
    )
    attn_gain_grad = jnp.sum(attn_grad * normed, axis=0)
    attn_shift_grad = jnp.sum(attn_grad, axis=0)
    mlp_gain_grad = jnp.sum(mlp_grad * normed, axis=0)
    mlp_shift_grad = jnp.sum(mlp_grad, axis=0)
    normed_grad = attn_grad * attn_gain + mlp_grad * mlp_gain
    key_weight_grad = inner_rows(attn_rows, key_low)
    key_bias_grad = jnp.sum(key_low, axis=0, dtype=jnp.float32)
    value_weight_grad = inner_rows(attn_rows, value_low)
    value_bias_grad = jnp.sum(value_low, axis=0, dtype=jnp.float32)
    input_grad = inv_std * (
        normed_grad
        - jnp.mean(normed_grad, axis=-1, keepdims=True)
        - normed * jnp.mean(normed_grad * normed, axis=-1, keepdims=True)
    )
    input_grad = (input_grad + grad_shard.astype(jnp.float32)).astype(jnp.bfloat16)
    (
        key_weight_grad,
        key_bias_grad,
        value_weight_grad,
        value_bias_grad,
        attn_gain_grad,
        attn_shift_grad,
        mlp_gain_grad,
        mlp_shift_grad,
        bias_grad,
    ) = lax.psum(
        (
            key_weight_grad,
            key_bias_grad,
            value_weight_grad,
            value_bias_grad,
            attn_gain_grad,
            attn_shift_grad,
            mlp_gain_grad,
            mlp_shift_grad,
            bias_grad,
        ),
        ("dp", "mp"),
    )
    (
        query_weight_grad,
        query_bias_grad,
        out_weight_grad,
        up_weight_grad,
        up_bias_grad,
        down_weight_grad,
    ) = lax.psum(
        (
            query_weight_grad,
            query_bias_grad,
            out_weight_grad,
            up_weight_grad,
            up_bias_grad,
            down_weight_grad,
        ),
        "dp",
    )
    return (
        block_out,
        input_grad,
        attn_gain_grad,
        attn_shift_grad,
        query_weight_grad,
        query_bias_grad,
        key_weight_grad,
        key_bias_grad,
        value_weight_grad,
        value_bias_grad,
        out_weight_grad,
        bias_grad,
        mlp_gain_grad,
        mlp_shift_grad,
        up_weight_grad,
        up_bias_grad,
        down_weight_grad,
        bias_grad,
    )


def solution(mesh):
    placed = (
        P(("dp", "mp"), None),
        P("dp", None),
        P(),
        P(),
        P(None, "mp"),
        P("mp"),
        P(),
        P(),
        P(),
        P(),
        P("mp", None),
        P(),
        P(),
        P(),
        P(None, "mp"),
        P("mp"),
        P("mp", None),
        P(),
        P(("dp", "mp"), None),
    )
    return jax.shard_map(
        per_device,
        mesh=mesh,
        in_specs=placed,
        out_specs=(
            P(("dp", "mp"), None),
            P(("dp", "mp"), None),
            P(),
            P(),
            P(None, "mp"),
            P("mp"),
            P(),
            P(),
            P(),
            P(),
            P("mp", None),
            P(),
            P(),
            P(),
            P(None, "mp"),
            P("mp"),
            P("mp", None),
            P(),
        ),
        check_vma=False,
    )
```

profile of v0, /device:TPU:0, one launch (start us, length us, event | category | flops | bytes accessed | tf_op | source)
XLA Modules:
  0.0 958.1 jit_solution(4647311742938053690)
XLA Ops:
  14.9 26.0 %all-gather.3.cloned.1.call-done = bf16[2048,768]{1,0:T(8,128)(2,1)} async-done(((bf16[512,768]{1,0:T(8,128)(2,1)}), bf16[2048,768]{1,0:T(8,128)(2,1)}) %all-gather.3.cloned.1.call-update) | async-done | bytes 3145744 | tf_op jit(solution)/shard_map/all_gather | solution.py:253
  53.2 96.5 %while.43 = (s32[]{:T(128)}, bf16[4,512,3,64]{1,3,2,0:T(8,128)(2,1)S(1)}, f32[4,3,512]{2,1,0:T(4,128)S(1)}, s32[4]{0:T(128)S(1)}, s32[1,2048]{1,0:T(1,128)S(1)},...) while((s32[]{:T(128)}, ...), condition=%wide.region_15.16_spmd, body=%wide.region_12.15_spmd.sunk | while | flops 846199808 | bytes 43135804 | solution.py:104
  159.1 181.0 %while.44 = (s32[]{:T(128)}, f32[4,512,3,64]{1,0,3,2:T(4,128)}, f32[4,2048,64]{1,2,0:T(8,128)}, f32[4,2048,64]{1,2,0:T(8,128)}, s32[4]{0:T(128)S(1)}, /*index=5*...) while((s32[]{:T(128)}, f32[4,512,3,64]{1,0,3,2:T(4,128)}, ...), condition=%wide.region_18.19_spmd, body=%wide.region_16.18_spmd.sunk | while | flops 2063825920 | bytes 182910384 | solution.py:145
  182.8 8.6 dynamic_update_slice.55
  196.3 8.3 fusion.252
  228.0 8.6 dynamic_update_slice.55
  241.5 8.3 fusion.252
  273.1 8.6 dynamic_update_slice.55
  286.7 8.3 fusion.252
  318.3 8.6 dynamic_update_slice.55
  331.8 8.3 fusion.252
  358.0 85.6 %while.42 = (s32[]{:T(128)}, bf16[4,512,3,64]{1,3,2,0:T(8,128)(2,1)}, s32[4]{0:T(128)S(1)}, s32[1,2048]{1,0:T(1,128)S(1)}, bf16[4,512,3,64]{1,3,2,0:T(8,128)(2,1...) while((s32[]{:T(128)}, ...), condition=%wide.region_8.9_spmd, body=%wide.region_5.8_spmd.sunk | while | flops 827329024 | bytes 28409132 | solution.py:104
  361.8 10.0 %fusion.232 = (f32[3,512]{1,0:T(4,128)S(1)}, f32[3,512,2048]{2,1,0:T(8,128)}) fusion(pred[512,2048]{1,0:T(8,128)(4,1)S(1)} %fusion.231, bf16[1,2048,64]{1,2,0:T(8,128)(2,1)S(1)} %get-tuple-element.756, bf16[4,512,3,64]{1,3,2,0:T(8,128)(2,1)} %get-tuple-element.755, s32[]{:T(128)} %get-tuple-element.738), kind=kOutput, calls=%fused_computation.219.clone.1 | convolution fusion | flops 415238144 | bytes 14096896 | tf_op jit(solution)/shard_map/while/body/eval_jaxpr/sub | solution.py:95
  371.8 7.6 fusion.233
  383.1 10.0 %fusion.232 = (f32[3,512]{1,0:T(4,128)S(1)}, f32[3,512,2048]{2,1,0:T(8,128)}) fusion(pred[512,2048]{1,0:T(8,128)(4,1)S(1)} %fusion.231, bf16[1,2048,64]{1,2,0:T(8,128)(2,1)S(1)} %get-tuple-element.756, bf16[4,512,3,64]{1,3,2,0:T(8,128)(2,1)} %get-tuple-element.755, s32[]{:T(128)} %get-tuple-element.738), kind=kOutput, calls=%fused_computation.219.clone.1 | convolution fusion | flops 415238144 | bytes 14096896 | tf_op jit(solution)/shard_map/while/body/eval_jaxpr/sub | solution.py:95
  393.2 7.6 fusion.233
  404.5 10.6 %fusion.232 = (f32[3,512]{1,0:T(4,128)S(1)}, f32[3,512,2048]{2,1,0:T(8,128)}) fusion(pred[512,2048]{1,0:T(8,128)(4,1)S(1)} %fusion.231, bf16[1,2048,64]{1,2,0:T(8,128)(2,1)S(1)} %get-tuple-element.756, bf16[4,512,3,64]{1,3,2,0:T(8,128)(2,1)} %get-tuple-element.755, s32[]{:T(128)} %get-tuple-element.738), kind=kOutput, calls=%fused_computation.219.clone.1 | convolution fusion | flops 415238144 | bytes 14096896 | tf_op jit(solution)/shard_map/while/body/eval_jaxpr/sub | solution.py:95
  426.3 10.0 %fusion.232 = (f32[3,512]{1,0:T(4,128)S(1)}, f32[3,512,2048]{2,1,0:T(8,128)}) fusion(pred[512,2048]{1,0:T(8,128)(4,1)S(1)} %fusion.231, bf16[1,2048,64]{1,2,0:T(8,128)(2,1)S(1)} %get-tuple-element.756, bf16[4,512,3,64]{1,3,2,0:T(8,128)(2,1)} %get-tuple-element.755, s32[]{:T(128)} %get-tuple-element.738), kind=kOutput, calls=%fused_computation.219.clone.1 | convolution fusion | flops 415238144 | bytes 14096896 | tf_op jit(solution)/shard_map/while/body/eval_jaxpr/sub | solution.py:95
  450.9 17.9 %convert_reduce_fusion.1 = (f32[768]{0:T(1024)S(1)}, bf16[2048,768]{1,0:T(8,128)(2,1)}, f32[2048,768]{1,0:T(8,128)S(1)}) fusion(f32[2048,768]{1,0:T(8,128)S(1)} %fusion.154, f32[768]{0:T(1024)S(1)} %copy-done.41, bf16[2048,768]{1,0:T(8,128)(2,1)S(1)} %copy-done.11, bf16[768,768]{1,0:T(8,128)(2,1)S(1)} %copy-done), kind=kOutput, calls=%fused_computation.108 | convolution fusion | flops 2533883136 | bytes 20060160 | tf_op jit(solution)/shard_map/dot_general | solution.py:60
  509.5 21.8 %all-reduce.2 = (f32[192]{0:T(256)}, f32[768]{0:T(1024)}) all-reduce(f32[192]{0:T(256)S(1)} %reduce_sum.233, f32[768]{0:T(1024)S(1)} %get-tuple-element.519), channel_id=1, replica_groups=mesh['dp'=8,'mp'=4] {'dp'}, use_global_device_ids=true, to_apply=%region_33.34 | all-reduce | flops 960 | bytes 7680 | tf_op jit(solution)/shard_map/psum | solution.py:365
  534.6 60.9 %reduce-scatter.14.cloned.1.call-done = f32[512,768]{1,0:T(8,128)} async-done(((f32[2048,768]{1,0:T(8,128)}), f32[512,768]{1,0:T(8,128)}) %reduce-scatter.14.cloned.1.call-update) | async-done | bytes 1572880 | tf_op jit(solution)/shard_map/reduce_scatter | solution.py:308
  601.1 40.1 %all-reduce = (f32[768]{0:T(1024)}, f32[768]{0:T(1024)}, f32[64]{0:T(128)}, f32[64]{0:T(128)}, f32[768]{0:T(1024)S(1)}, /*index=5*/f32[768]{0:T(1024)}, f32[768]{0:T(1024)}) all-reduce(f32[768]{0:T(1024)S(1)} %get-tuple-element.536, f32[768]{0:T(1024)S(1)} %get-tuple-element.537, ...), channel_id=1, replica_groups=mesh['dp'=8,'mp'=4] {'dp','mp'}, use_global_device_ids=true, to_apply=%region_28.29 | all-reduce | flops 3968 | bytes 31744 | tf_op jit(solution)/shard_map/psum | solution.py:344
  644.1 87.1 %all-reduce.7.cloned.1.call-done = (f32[768,64]{0,1:T(8,128)}, f32[768,64]{0,1:T(8,128)}) async-done(((f32[768,64]{0,1:T(8,128)}, f32[768,64]{0,1:T(8,128)}), (f32[768,64]{0,1:T(8,128)}, f32[768,64]{0,1:T(8,128)})) %all-reduce.7.cloned.1.call-update) | async-done | bytes 393232 | tf_op jit(solution)/shard_map/psum | solution.py:344
  731.2 207.5 %all-reduce.9.cloned.1.call-done = (f32[768,192]{0,1:T(8,128)}, f32[192,768]{1,0:T(8,128)}, f32[768,768]{1,0:T(8,128)}, f32[768,768]{1,0:T(8,128)}) async-done(((f32[768,192]{0,1:T(8,128)}, f32[192,768]{1,0:T(8,128)}, f32[768,768]{1,0:T(8,128)}, f32[768,768]{1,0:T(8,128)}), (f32[768,192]{0,1:T(8,128)}, f32[192,768]{1,0:T(8,128)}, f32[768,768]{1,0:T(8,128)}, ...) | async-done | bytes 5898256 | tf_op jit(solution)/shard_map/psum | solution.py:365
  (323 shorter events, 333.6 us)
Async XLA Ops:
  7.2 443.7 %copy-start = (bf16[768,768]{1,0:T(8,128)(2,1)S(1)}, bf16[768,768]{1,0:T(8,128)(2,1)}, u32[]{:S(2)}) copy-start(bf16[768,768]{1,0:T(8,128)(2,1)} %param.41) | copy-start | bytes 3538948
  7.2 33.7 %all-gather.3.cloned.1.call-start = ((), (), s32[]{:S(2)}) async-start(), calls=%async_computation.5 | async-start | bytes 3932160 | tf_op jit(solution)/shard_map/all_gather | solution.py:253
  8.0 141.8 %all-gather.5.cloned.1.call-start = ((), (), s32[]{:S(2)}) async-start(), calls=%async_computation.7 | async-start | bytes 3932160 | tf_op jit(solution)/shard_map/all_gather | solution.py:280
  11.9 488.8 %reduce-scatter.10.cloned.1.call-start = ((), (), s32[]{:S(2)}) async-start(), calls=%async_computation.9 | async-start | bytes 655360 | tf_op jit(solution)/shard_map/reduce_scatter | solution.py:309
  53.1 96.6 %copy-start.28 = (bf16[192,768]{1,0:T(8,128)(2,1)S(1)}, bf16[192,768]{1,0:T(8,128)(2,1)}, u32[]{:S(2)}) copy-start(bf16[192,768]{1,0:T(8,128)(2,1)} %param.35) | copy-start | bytes 884740
  159.1 182.9 %copy-start.33 = (f32[2048]{0:T(1024)S(1)}, f32[2048]{0:T(1024)}, u32[]{:S(2)}) copy-start(f32[2048]{0:T(1024)} %copy-done.32) | copy-start | bytes 24580
  159.1 182.9 %copy-start.48 = (f32[8]{0:T(128)S(1)}, f32[8]{0:T(128)}, u32[]{:S(2)}) copy-start(f32[8]{0:T(128)} %copy-done.47) | copy-start | bytes 100
  343.2 159.7 %reduce-scatter.12.cloned.1.call-start = ((), (), s32[]{:S(2)}) async-start(), calls=%async_computation.10 | async-start | bytes 655360 | tf_op jit(solution)/shard_map/reduce_scatter | solution.py:310
  345.8 187.3 %reduce-scatter.8.cloned.1.call-start = ((), (), s32[]{:S(2)}) async-start(), calls=%async_computation.8 | async-start | bytes 7864320 | tf_op jit(solution)/shard_map/reduce_scatter | solution.py:307
  357.0 177.6 %reduce-scatter.6.cloned.1.call-start = ((), (), s32[]{:S(2)}) async-start(), calls=%async_computation.6 | async-start | bytes 7864320 | tf_op jit(solution)/shard_map/reduce_scatter | solution.py:256
  358.0 87.5 %copy-start.31 = (f32[2048]{0:T(1024)S(1)}, f32[2048]{0:T(1024)}, u32[]{:S(2)}) copy-start(f32[2048]{0:T(1024)} %copy-done.30) | copy-start | bytes 24580
  358.0 87.6 %copy-start.35 = (f32[2048]{0:T(1024)S(1)}, f32[2048]{0:T(1024)}, u32[]{:S(2)}) copy-start(f32[2048]{0:T(1024)} %copy-done.34) | copy-start | bytes 24580
  358.0 87.6 %copy-start.42 = (f32[768]{0:T(1024)S(1)}, f32[768]{0:T(1024)}, u32[]{:S(2)}) copy-start(f32[768]{0:T(1024)} %param.37) | copy-start | bytes 9220
  358.0 87.6 %copy-start.50 = (f32[768]{0:T(1024)S(1)}, f32[768]{0:T(1024)}, u32[]{:S(2)}) copy-start(f32[768]{0:T(1024)} %param.38) | copy-start | bytes 9220
  476.3 119.2 %reduce-scatter.14.cloned.1.call-start = ((), (), s32[]{:S(2)}) async-start(), calls=%async_computation.11 | async-start | bytes 7864320 | tf_op jit(solution)/shard_map/reduce_scatter | solution.py:308
  485.1 246.1 %all-reduce.7.cloned.1.call-start = ((), (), s32[]{:S(2)}) async-start(), calls=%async_computation.12 | async-start | bytes 786432 | tf_op jit(solution)/shard_map/psum | solution.py:344
  505.1 433.7 %all-reduce.9.cloned.1.call-start = ((), (), s32[]{:S(2)}) async-start(), calls=%async_computation.13 | async-start | bytes 11796480 | tf_op jit(solution)/shard_map/psum | solution.py:365
  505.1 90.4 %copy-start.25 = (bf16[768,64]{0,1:T(8,128)(2,1)S(1)}, bf16[768,64]{0,1:T(8,128)(2,1)}, u32[]{:S(2)}) copy-start(bf16[768,64]{0,1:T(8,128)(2,1)} %param.33) | copy-start | bytes 294916
  505.1 90.4 %copy-start.37 = (f32[768]{0:T(1024)S(1)}, f32[768]{0:T(1024)}, u32[]{:S(2)}) copy-start(f32[768]{0:T(1024)} %param.27) | copy-start | bytes 9220
  505.1 90.4 %copy-start.43 = (f32[768]{0:T(1024)S(1)}, f32[768]{0:T(1024)}, u32[]{:S(2)}) copy-start(f32[768]{0:T(1024)} %param.42) | copy-start | bytes 9220
  505.2 90.4 %copy-start.44 = (f32[768]{0:T(1024)S(1)}, f32[768]{0:T(1024)}, u32[]{:S(2)}) copy-start(f32[768]{0:T(1024)} %param.36) | copy-start | bytes 9220
  509.0 92.1 %copy-start.38 = (f32[768]{0:T(1024)S(1)}, f32[768]{0:T(1024)}, u32[]{:S(2)}) copy-start(f32[768]{0:T(1024)} %get-tuple-element.524) | copy-start | bytes 9220
  509.0 132.1 %copy-start.10 = (bf16[512,768]{1,0:T(8,128)(2,1)S(1)}, bf16[512,768]{1,0:T(8,128)(2,1)}, u32[]{:S(2)}) copy-start(bf16[512,768]{1,0:T(8,128)(2,1)} %get-tuple-element.525) | copy-start | bytes 2359300
  641.2 310.0 %copy-start.46 = (f32[768]{0:T(1024)}, f32[768]{0:T(1024)S(1)}, u32[]{:S(2)}) copy-start(f32[768]{0:T(1024)S(1)} %get-tuple-element.904) | copy-start | bytes 9220
  (46 other events, 517.7 us)
Sparse Core Ops, SparseCore 0:
  9.6 31.2 all-gather.2
  43.0 28.5 all-gather.4
  343.3 21.6 reduce-scatter.9
  368.0 21.6 reduce-scatter.11
  392.1 58.4 reduce-scatter.7
  476.5 58.0 reduce-scatter.5
  537.1 58.3 reduce-scatter.13
  603.1 128.1 all-reduce.6
  737.0 201.6 all-reduce.8
where the time goes:
time: 964 us; the launch traced here: 958 us
  waiting for transfers between devices  384 us (40%)
  matrix products  296 us (31%)
  other arithmetic  90.6 us (9%)
  local copies, waits for them, and re-layouts  85.2 us (9%)
  blocking collectives  61.9 us (6%)
  loops' own time  24.6 us (3%)
  between operations  15.1 us (2%)
    psum x1, waiting for transfers between devices, per_device(): lax.psum((query_weight_grad, query_bias_grad, out_weight_grad, up_weight_...  208 us
    psum x1, waiting for transfers between devices, per_device(): lax.psum((key_weight_grad, key_bias_grad, value_weight_grad, value_bias_g...  87.1 us
    reduce_scatter x1, waiting for transfers between devices, per_device(): lax.psum_scatter(mlp_part, 'mp', scatter_dimension=0, tiled=True)  60.9 us
    dot_general x8, matrix products, one_block(): jnp.einsum('hbk,ke->bhe', probs_low, value_row, preferred_element_type=jn...  56.8 us
    sub x4, matrix products, one_block(): expo = jnp.exp(scores - peak)  40.6 us
    dot_general x6, matrix products, times_transposed(): lax.dot_general(left, right, (((1,), (1,)), ((), ())), preferred_element_...  40.4 us
    psum x1, blocking collectives, per_device(): lax.psum((key_weight_grad, key_bias_grad, value_weight_grad, value_bias_g...  40.1 us
    dot_general x8, matrix products, block_scores(): jnp.einsum('bhe,ke->hbk', query_block, key_row, preferred_element_type=jn...  38.3 us
  transfers between devices with their start and end apart: 9, of which 5 were waited for; matrix products, arithmetic and copies ran while one was open for 28% of the time, Pallas kernels for 0%

commit v1 on v0

--- a/solution.py
+++ b/solution.py
@@ -9,6 +9,11 @@
 SLOT = 2048
 DOCS = 4
 epsilon = 1e-05
+
+
+def by_each_axis(array, axis_one, axis_two):
+    inner = lax.psum(array, axis_one)
+    return lax.psum(inner, axis_two)
 
 
 def normalize(values):
@@ -341,7 +346,7 @@
         mlp_gain_grad,
         mlp_shift_grad,
         bias_grad,
-    ) = lax.psum(
+    ) = by_each_axis(
         (
             key_weight_grad,
             key_bias_grad,
@@ -353,7 +358,8 @@
             mlp_shift_grad,
             bias_grad,
         ),
-        ("dp", "mp"),
+        "mp",
+        "dp",
     )
     (
         query_weight_grad,

time: 964 us -> 884 us (0.917)
  waiting for transfers between devices: 384 us -> 317 us
  blocking collectives: 61.9 us -> 50.2 us
    psum x1, waiting for transfers between devices: 87.1 us -> 0.02 us  [by_each_axis(): inner = lax.psum(array, axis_one)]
    psum x1, waiting for transfers between devices: 208 us -> 165 us  [per_device(): lax.psum((query_weight_grad, query_bias_grad, out_weight_grad, up_weight_...]
    reduce_scatter x1, waiting for transfers between devices: 1.49 us -> 29.3 us  [per_device(): lax.psum_scatter(jnp.dot(context_fwd, out_weight, preferred_element_type=...]
    reduce_scatter x1, waiting for transfers between devices: 0.01 us -> 22.6 us  [per_device(): lax.psum_scatter(value_part, 'mp', scatter_dimension=0, tiled=True)]
    reduce_scatter x1, waiting for transfers between devices: 0.01 us -> 12.5 us  [per_device(): lax.psum_scatter(key_part, 'mp', scatter_dimension=0, tiled=True)]
    psum x2, blocking collectives: 61.9 us -> 50.2 us  [the longest x1 40 us: by_each_axis(): return lax.psum(inner, axis_two)]
  transfers between devices with their start and end apart: 9 -> 9, of which waited for: 5 -> 6; matrix products, arithmetic and copies ran while one was open for 28% -> 30% of each run, Pallas kernels for 0% -> 0%
where the time goes in v1:
time: 884 us; the launch traced here: 878 us
  waiting for transfers between devices  317 us (36%)
  matrix products  294 us (33%)
  other arithmetic  90.5 us (10%)
  local copies, waits for them, and re-layouts  85.3 us (10%)
  blocking collectives  50.2 us (6%)
  loops' own time  24.6 us (3%)
  between operations  15.1 us (2%)
    psum x1, waiting for transfers between devices, per_device(): lax.psum((query_weight_grad, query_bias_grad, out_weight_grad, up_weight_...  165 us
    reduce_scatter x1, waiting for transfers between devices, per_device(): lax.psum_scatter(mlp_part, 'mp', scatter_dimension=0, tiled=True)  61.1 us
    dot_general x8, matrix products, one_block(): jnp.einsum('hbk,ke->bhe', probs_low, value_row, preferred_element_type=jn...  58 us
    dot_general x6, matrix products, times_transposed(): lax.dot_general(left, right, (((1,), (1,)), ((), ())), preferred_element_...  40.1 us
    psum x1, blocking collectives, by_each_axis(): return lax.psum(inner, axis_two)  40 us
    sub x4, matrix products, one_block(): expo = jnp.exp(scores - peak)  39.9 us
    dot_general x8, matrix products, block_scores(): jnp.einsum('bhe,ke->hbk', query_block, key_row, preferred_element_type=jn...  38.3 us
    dynamic_update_slice x8, local copies, waits for them, and re-layouts, attend_forward(): lax.map(one_block, (queries.reshape(groups * block_count, block_rows, hea...  36.1 us
  transfers between devices with their start and end apart: 9, of which 6 were waited for; matrix products, arithmetic and copies ran while one was open for 30% of the time, Pallas kernels for 0%

profile of v1, /device:TPU:0, one launch (start us, length us, event | category | flops | bytes accessed | tf_op | source)
XLA Modules:
  0.0 878.1 jit_solution(11320731077645990109)
XLA Ops:
  14.9 26.0 %all-gather.3.cloned.1.call-done = bf16[2048,768]{1,0:T(8,128)(2,1)} async-done(((bf16[512,768]{1,0:T(8,128)(2,1)}), bf16[2048,768]{1,0:T(8,128)(2,1)}) %all-gather.3.cloned.1.call-update) | async-done | bytes 3145744 | tf_op jit(solution)/shard_map/all_gather | solution.py:258
  53.2 96.5 %while.43 = (s32[]{:T(128)}, bf16[4,512,3,64]{1,3,2,0:T(8,128)(2,1)S(1)}, f32[4,3,512]{2,1,0:T(4,128)S(1)}, s32[4]{0:T(128)S(1)}, s32[1,2048]{1,0:T(1,128)S(1)},...) while((s32[]{:T(128)}, ...), condition=%wide.region_15.16_spmd, body=%wide.region_12.15_spmd.sunk | while | flops 846199808 | bytes 43135804 | solution.py:109
  159.1 181.0 %while.44 = (s32[]{:T(128)}, f32[4,512,3,64]{1,0,3,2:T(4,128)}, f32[4,2048,64]{1,2,0:T(8,128)}, f32[4,2048,64]{1,2,0:T(8,128)}, s32[4]{0:T(128)S(1)}, /*index=5*...) while((s32[]{:T(128)}, f32[4,512,3,64]{1,0,3,2:T(4,128)}, ...), condition=%wide.region_18.19_spmd, body=%wide.region_16.18_spmd.sunk | while | flops 2063825920 | bytes 182910384 | solution.py:150
  182.8 8.6 dynamic_update_slice.55
  196.3 8.3 fusion.252
  228.0 8.6 dynamic_update_slice.55
  241.5 8.3 fusion.252
  273.1 8.6 dynamic_update_slice.55
  318.3 8.6 dynamic_update_slice.55
  331.8 8.3 fusion.252
  352.4 12.5 %reduce-scatter.10.cloned.1.call-done = f32[512,64]{0,1:T(8,128)} async-done(((f32[2048,64]{0,1:T(8,128)}), f32[512,64]{0,1:T(8,128)}) %reduce-scatter.10.cloned.1.call-update) | async-done | bytes 131088 | tf_op jit(solution)/shard_map/reduce_scatter | solution.py:314
  367.1 22.6 %reduce-scatter.12.cloned.1.call-done = f32[512,64]{0,1:T(8,128)} async-done(((f32[2048,64]{0,1:T(8,128)}), f32[512,64]{0,1:T(8,128)}) %reduce-scatter.12.cloned.1.call-update) | async-done | bytes 131088 | tf_op jit(solution)/shard_map/reduce_scatter | solution.py:315
  396.6 86.1 %while.42 = (s32[]{:T(128)}, bf16[4,512,3,64]{1,3,2,0:T(8,128)(2,1)}, s32[4]{0:T(128)S(1)}, s32[1,2048]{1,0:T(1,128)S(1)}, bf16[4,512,3,64]{1,3,2,0:T(8,128)(2,1...) while((s32[]{:T(128)}, ...), condition=%wide.region_8.9_spmd, body=%wide.region_5.8_spmd.sunk | while | flops 827329024 | bytes 28409132 | solution.py:109
  400.4 10.0 %fusion.232 = (f32[3,512]{1,0:T(4,128)S(1)}, f32[3,512,2048]{2,1,0:T(8,128)}) fusion(pred[512,2048]{1,0:T(8,128)(4,1)S(1)} %fusion.231, bf16[1,2048,64]{1,2,0:T(8,128)(2,1)S(1)} %get-tuple-element.765, bf16[4,512,3,64]{1,3,2,0:T(8,128)(2,1)} %get-tuple-element.764, s32[]{:T(128)} %get-tuple-element.747), kind=kOutput, calls=%fused_computation.219.clone.1 | convolution fusion | flops 415238144 | bytes 14096896 | tf_op jit(solution)/shard_map/while/body/eval_jaxpr/sub | solution.py:100
  421.5 10.0 %fusion.232 = (f32[3,512]{1,0:T(4,128)S(1)}, f32[3,512,2048]{2,1,0:T(8,128)}) fusion(pred[512,2048]{1,0:T(8,128)(4,1)S(1)} %fusion.231, bf16[1,2048,64]{1,2,0:T(8,128)(2,1)S(1)} %get-tuple-element.765, bf16[4,512,3,64]{1,3,2,0:T(8,128)(2,1)} %get-tuple-element.764, s32[]{:T(128)} %get-tuple-element.747), kind=kOutput, calls=%fused_computation.219.clone.1 | convolution fusion | flops 415238144 | bytes 14096896 | tf_op jit(solution)/shard_map/while/body/eval_jaxpr/sub | solution.py:100
  431.5 8.9 %fusion.233 = bf16[4,512,3,64]{1,3,2,0:T(8,128)(2,1)} fusion(bf16[4,512,3,64]{1,3,2,0:T(8,128)(2,1)} %get-tuple-element.748, s32[]{:T(128)} %get-tuple-element.747, f32[3,512,2048]{2,1,0:T(8,128)} %get-tuple-element.709, f32[3,512]{1,0:T(4,128)S(1)} %get-tuple-element.710, bf16[1,2048,64]{1,2,0:T(8,128)(2,1)S(1)} %get-tuple-element.766), kind=kOutput, calls=%fused_computation.15.clone.1 | convolution fusion | flops 408944640 | bytes 13244928 | tf_op jit(solution)/shard_map/while/body/eval_jaxpr/hbk,ke->bhe/dot_general | solution.py:103
  444.1 10.0 %fusion.232 = (f32[3,512]{1,0:T(4,128)S(1)}, f32[3,512,2048]{2,1,0:T(8,128)}) fusion(pred[512,2048]{1,0:T(8,128)(4,1)S(1)} %fusion.231, bf16[1,2048,64]{1,2,0:T(8,128)(2,1)S(1)} %get-tuple-element.765, bf16[4,512,3,64]{1,3,2,0:T(8,128)(2,1)} %get-tuple-element.764, s32[]{:T(128)} %get-tuple-element.747), kind=kOutput, calls=%fused_computation.219.clone.1 | convolution fusion | flops 415238144 | bytes 14096896 | tf_op jit(solution)/shard_map/while/body/eval_jaxpr/sub | solution.py:100
  465.2 10.0 %fusion.232 = (f32[3,512]{1,0:T(4,128)S(1)}, f32[3,512,2048]{2,1,0:T(8,128)}) fusion(pred[512,2048]{1,0:T(8,128)(4,1)S(1)} %fusion.231, bf16[1,2048,64]{1,2,0:T(8,128)(2,1)S(1)} %get-tuple-element.765, bf16[4,512,3,64]{1,3,2,0:T(8,128)(2,1)} %get-tuple-element.764, s32[]{:T(128)} %get-tuple-element.747), kind=kOutput, calls=%fused_computation.219.clone.1 | convolution fusion | flops 415238144 | bytes 14096896 | tf_op jit(solution)/shard_map/while/body/eval_jaxpr/sub | solution.py:100
  489.9 17.9 %convert_reduce_fusion.1 = (f32[768]{0:T(1024)S(1)}, bf16[2048,768]{1,0:T(8,128)(2,1)}, f32[2048,768]{1,0:T(8,128)S(1)}) fusion(f32[2048,768]{1,0:T(8,128)S(1)} %fusion.154, f32[768]{0:T(1024)S(1)} %copy-done.41, bf16[2048,768]{1,0:T(8,128)(2,1)S(1)} %copy-done.11, bf16[768,768]{1,0:T(8,128)(2,1)S(1)} %copy-done), kind=kOutput, calls=%fused_computation.108 | convolution fusion | flops 2533883136 | bytes 20060160 | tf_op jit(solution)/shard_map/dot_general | solution.py:65
  544.8 29.3 %reduce-scatter.6.cloned.1.call-done = f32[512,768]{1,0:T(8,128)} async-done(((f32[2048,768]{1,0:T(8,128)}), f32[512,768]{1,0:T(8,128)}) %reduce-scatter.6.cloned.1.call-update) | async-done | bytes 1572880 | tf_op jit(solution)/shard_map/reduce_scatter | solution.py:261
  574.1 61.1 %reduce-scatter.14.cloned.1.call-done = f32[512,768]{1,0:T(8,128)} async-done(((f32[2048,768]{1,0:T(8,128)}), f32[512,768]{1,0:T(8,128)}) %reduce-scatter.14.cloned.1.call-update) | async-done | bytes 1572880 | tf_op jit(solution)/shard_map/reduce_scatter | solution.py:313
  640.7 10.2 %all-reduce.2 = (f32[768]{0:T(1024)S(1)}, f32[768]{0:T(1024)S(1)}, f32[64]{0:T(128)S(1)}, f32[64]{0:T(128)S(1)}, f32[768]{0:T(1024)S(1)}, /*index=5*/f32[768]{0:T(1024)S(1)}, f32[768]{0:T(1024)S(1)}) all-reduce(f32[768]{0:T(1024)S(1)} %get-tuple-element.545, f32[768]{0:T(1024)S(1)} %get-tuple-element.546, ...), channel_id=1, replica_groups=mesh['dp'=8,'mp'=4] {'mp'}, use_global_device_ids=true, to_apply=%region_28.29 | all-reduce | flops 3968 | bytes 31744 | tf_op jit(solution)/shard_map/psum | solution.py:15
  651.0 40.0 %all-reduce = (f32[768]{0:T(1024)}, f32[768]{0:T(1024)}, f32[192]{0:T(256)}, f32[64]{0:T(128)}, f32[64]{0:T(128)}, /*index=5*/f32[768]{0:T(1024)S(1)}, f32[768]{0:T(1024)}, f32[768]{0:T(1024)}, f32[768]{0:T(1024)}) all-reduce(f32[768]{0:T(1024)S(1)} %get-tuple-element.519, ...), channel_id=1, replica_groups=mesh['dp'=8,'mp'=4] {'dp'}, use_global_device_ids=true, to_apply=%region_29.30 | all-reduce | flops 4928 | bytes 39424 | tf_op jit(solution)/shard_map/psum | solution.py:16
  693.9 164.8 %all-reduce.7.cloned.1.call-done = (f32[768,192]{0,1:T(8,128)}, f32[768,64]{0,1:T(8,128)}, f32[768,64]{0,1:T(8,128)}, f32[192,768]{1,0:T(8,128)}, f32[768,768]{1,0:T(8,128)}, /*index=5*/f32[768,768]{1,0:T(8,128)}) async-done(((f32[768,192]{0,1:T(8,128)}, f32[768,64]{0,1:T(8,128)}, f32[768,64]{0,1:T(8,128)}, f32[192,768]{1,0:T(8,128)}, f32[768,768]{1,0:T(8,128)}, /*index=5*/f32[768,768]{1,0:T(8,128)}), ...) | async-done | bytes 6291472 | tf_op jit(solution)/shard_map/psum | solution.py:371
  (323 shorter events, 345.8 us)
Async XLA Ops:
  7.2 482.7 %copy-start = (bf16[768,768]{1,0:T(8,128)(2,1)S(1)}, bf16[768,768]{1,0:T(8,128)(2,1)}, u32[]{:S(2)}) copy-start(bf16[768,768]{1,0:T(8,128)(2,1)} %param.41) | copy-start | bytes 3538948
  7.2 33.7 %all-gather.3.cloned.1.call-start = ((), (), s32[]{:S(2)}) async-start(), calls=%async_computation.5 | async-start | bytes 3932160 | tf_op jit(solution)/shard_map/all_gather | solution.py:258
  8.0 141.7 %all-gather.5.cloned.1.call-start = ((), (), s32[]{:S(2)}) async-start(), calls=%async_computation.7 | async-start | bytes 3932160 | tf_op jit(solution)/shard_map/all_gather | solution.py:285
  11.9 353.0 %reduce-scatter.10.cloned.1.call-start = ((), (), s32[]{:S(2)}) async-start(), calls=%async_computation.9 | async-start | bytes 655360 | tf_op jit(solution)/shard_map/reduce_scatter | solution.py:314
  53.1 96.6 %copy-start.28 = (bf16[192,768]{1,0:T(8,128)(2,1)S(1)}, bf16[192,768]{1,0:T(8,128)(2,1)}, u32[]{:S(2)}) copy-start(bf16[192,768]{1,0:T(8,128)(2,1)} %param.35) | copy-start | bytes 884740
  159.1 182.8 %copy-start.33 = (f32[2048]{0:T(1024)S(1)}, f32[2048]{0:T(1024)}, u32[]{:S(2)}) copy-start(f32[2048]{0:T(1024)} %copy-done.32) | copy-start | bytes 24580
  159.1 182.9 %copy-start.48 = (f32[8]{0:T(128)S(1)}, f32[8]{0:T(128)}, u32[]{:S(2)}) copy-start(f32[8]{0:T(128)} %copy-done.47) | copy-start | bytes 100
  343.1 46.5 %reduce-scatter.12.cloned.1.call-start = ((), (), s32[]{:S(2)}) async-start(), calls=%async_computation.10 | async-start | bytes 655360 | tf_op jit(solution)/shard_map/reduce_scatter | solution.py:315
  345.7 195.5 %all-reduce.9.cloned.1.call-start = ((), (), s32[]{:S(2)}) async-start(), calls=%async_computation.13 | async-start | bytes 786432 | tf_op jit(solution)/shard_map/psum | solution.py:15
  391.8 152.9 %reduce-scatter.8.cloned.1.call-start = ((), (), s32[]{:S(2)}) async-start(), calls=%async_computation.8 | async-start | bytes 7864320 | tf_op jit(solution)/shard_map/reduce_scatter | solution.py:312
  395.6 178.5 %reduce-scatter.6.cloned.1.call-start = ((), (), s32[]{:S(2)}) async-start(), calls=%async_computation.6 | async-start | bytes 7864320 | tf_op jit(solution)/shard_map/reduce_scatter | solution.py:261
  396.6 88.0 %copy-start.31 = (f32[2048]{0:T(1024)S(1)}, f32[2048]{0:T(1024)}, u32[]{:S(2)}) copy-start(f32[2048]{0:T(1024)} %copy-done.30) | copy-start | bytes 24580
  396.6 88.0 %copy-start.35 = (f32[2048]{0:T(1024)S(1)}, f32[2048]{0:T(1024)}, u32[]{:S(2)}) copy-start(f32[2048]{0:T(1024)} %copy-done.34) | copy-start | bytes 24580
  396.6 88.0 %copy-start.42 = (f32[768]{0:T(1024)S(1)}, f32[768]{0:T(1024)}, u32[]{:S(2)}) copy-start(f32[768]{0:T(1024)} %param.37) | copy-start | bytes 9220
  396.6 88.0 %copy-start.50 = (f32[768]{0:T(1024)S(1)}, f32[768]{0:T(1024)}, u32[]{:S(2)}) copy-start(f32[768]{0:T(1024)} %param.38) | copy-start | bytes 9220
  515.4 119.8 %reduce-scatter.14.cloned.1.call-start = ((), (), s32[]{:S(2)}) async-start(), calls=%async_computation.11 | async-start | bytes 7864320 | tf_op jit(solution)/shard_map/reduce_scatter | solution.py:313
  523.9 334.7 %all-reduce.7.cloned.1.call-start = ((), (), s32[]{:S(2)}) async-start(), calls=%async_computation.12 | async-start | bytes 12582912 | tf_op jit(solution)/shard_map/psum | solution.py:371
  541.2 94.0 %copy-start.25 = (bf16[768,64]{0,1:T(8,128)(2,1)S(1)}, bf16[768,64]{0,1:T(8,128)(2,1)}, u32[]{:S(2)}) copy-start(bf16[768,64]{0,1:T(8,128)(2,1)} %param.33) | copy-start | bytes 294916
  541.2 94.0 %copy-start.37 = (f32[768]{0:T(1024)S(1)}, f32[768]{0:T(1024)}, u32[]{:S(2)}) copy-start(f32[768]{0:T(1024)} %param.27) | copy-start | bytes 9220
  541.2 93.9 %copy-start.43 = (f32[768]{0:T(1024)S(1)}, f32[768]{0:T(1024)}, u32[]{:S(2)}) copy-start(f32[768]{0:T(1024)} %param.42) | copy-start | bytes 9220
  541.2 93.9 %copy-start.44 = (f32[768]{0:T(1024)S(1)}, f32[768]{0:T(1024)}, u32[]{:S(2)}) copy-start(f32[768]{0:T(1024)} %param.36) | copy-start | bytes 9220
  542.5 98.2 %copy-start.38 = (f32[768]{0:T(1024)S(1)}, f32[768]{0:T(1024)}, u32[]{:S(2)}) copy-start(f32[768]{0:T(1024)} %get-tuple-element.533) | copy-start | bytes 9220
  542.5 148.5 %copy-start.10 = (bf16[512,768]{1,0:T(8,128)(2,1)S(1)}, bf16[512,768]{1,0:T(8,128)(2,1)}, u32[]{:S(2)}) copy-start(bf16[512,768]{1,0:T(8,128)(2,1)} %get-tuple-element.534) | copy-start | bytes 2359300
  691.0 180.1 %copy-start.46 = (f32[768]{0:T(1024)}, f32[768]{0:T(1024)S(1)}, u32[]{:S(2)}) copy-start(f32[768]{0:T(1024)S(1)} %get-tuple-element.913) | copy-start | bytes 9220
  (46 other events, 515.9 us)
Sparse Core Ops, SparseCore 0:
  9.6 31.2 all-gather.2
  43.0 28.5 all-gather.4
  343.2 21.6 reduce-scatter.9
  368.0 21.6 reduce-scatter.11
  393.0 32.7 all-reduce.8
  428.3 58.3 reduce-scatter.7
  515.5 58.4 reduce-scatter.5
  576.7 58.3 reduce-scatter.13
  642.1 216.5 all-reduce.6
